TPU v7x, 32 devices: a whole 2x2x4 slice. The times are simulated.
32 devices in a mesh: dp: 4 (over z), seq: 8 (over y, x, core).
Axes of the slice: x: 2, y: 2, z: 4, core: 2. Of those that a mesh axis runs over, the one named last changes fastest.
Arguments:
- frames_in: bfloat16 [4, 4096, 1024], P('dp', 'seq'), may hold values from -16 to 16
- memory_in: bfloat16 [4, 32, 1024], P('dp', 'seq'), may hold values from -6 to 6
- w_query: bfloat16 [1024, 1024], P(None, 'dp'), may hold values from -1 to 1
- w_key: bfloat16 [1024, 1024], P(None, 'dp'), may hold values from -1 to 1
- w_value: bfloat16 [1024, 1024], P(None, 'dp'), may hold values from -0.1875 to 0.1875
- lengths: int32 [4], P('dp'), may hold values from 1024 to 4096, as said below
Outputs:
- context: bfloat16 [4, 4096, 1024], P('dp', 'seq')
- memory_out: bfloat16 [4, 32, 1024], P('dp', 'seq')
Inputs may be any that keep to these rules, and one draw needn't show every extreme that they name: `lengths`: some utterance has all 4096 frames live; every utterance has at least a quarter of them.
All inputs are finite; a program needn't handle non-finite values.
Results may differ from a plain program's by a relative error of at most 0.0071.
Values may be sent and summed in bfloat16 or wider, within the bound.
No kernel may reach another device: no remote copies, remote signals or barrier semaphores. Data moves between devices by JAX's collectives and lax.ppermute only.
A program may use at most 64 MiB of HBM per device.

v0:
```python
import math

import jax
import jax.numpy as jnp
from jax import lax
from jax.experimental import pallas as pl
from jax.experimental.pallas import tpu as pltpu
from jax.sharding import PartitionSpec as P


HEADS = 16
LEFT = 128
RIGHT = 32
LANES = 128
PAD_ROWS = 16
DEAD = -1e30
MIB = 1024 * 1024


def shifted(block, axis, distance):
    count = lax.axis_size(axis)
    route = [(i - distance, i) for i in range(count) if 0 <= i - distance < count]
    return lax.ppermute(block, axis, route)


def swapped(block, axis, masks):
    count = lax.axis_size(axis)
    return lax.ppermute(block, axis, [(i, i ^ masks[i % 2]) for i in range(count)])


def stage_masks(count):
    bits = [1 << b for b in range(1, count.bit_length() - 1)]
    turned = bits[1:] + bits[:1]
    return [pair for pair in zip(bits, turned)] + [(1, 1)]


def joined(parts):
    rows = sum(p.shape[0] for p in parts)
    out = jnp.zeros((rows,) + parts[0].shape[1:], parts[0].dtype)
    at = 0
    for p in parts:
        out = lax.dynamic_update_slice_in_dim(out, p, at, 0)
        at += p.shape[0]
    return out


def gather_slices(mine, axis, tail=None, got=None):
    (even_a, odd_a), (even_b, odd_b) = stage_masks(lax.axis_size(axis))[:2]
    size = mine.shape[0]
    sent = mine if tail is None else joined([mine, *tail])
    if got is None:
        got = swapped(sent, axis, (even_a, odd_a))
    both = [mine, got] if tail is None else [mine, got[:size], *tail, got[size:]]
    held = joined(both)
    other = swapped(held, axis, (even_b, odd_b))
    pair_held = swapped(held, axis, (1, 1))
    pair_other = swapped(other, axis, (1, 1))
    slots = [(0, 0), (even_a, odd_a), (even_b, odd_b), (even_a ^ even_b, odd_a ^ odd_b)]
    slots += [(o ^ 1, e ^ 1) for e, o in slots]
    return [held, other, pair_held, pair_other], slots, got


def gather_bank(memory_in, axis):
    count = lax.axis_size(axis)
    bank = memory_in
    bit = 1
    while bit < count:
        bank = jnp.concatenate([bank, swapped(bank, axis, (bit, bit))], axis=1)
        bit *= 2
    return bank


def cut(ids, part, frames_in, memory_in, weights):
    _, rows, feat = frames_in.shape
    segs = memory_in.shape[1]
    cols = weights[0].shape[1]
    groups = feat // cols

    def kernel(ids_ref, f_ref, m_ref, *refs):
        w_refs = refs[:3]
        u_ref, near_ref, far_ref, bank_ref, m_scr, sem = refs[3:]
        at = pl.multiple_of(ids_ref[0] * part, part)
        odd = ids_ref[0] % 2
        top = pl.multiple_of((rows - LEFT) * odd, PAD_ROWS)
        end = pl.multiple_of((rows - LEFT) * (1 - odd), PAD_ROWS)
        copies = [pltpu.make_async_copy(m_ref.at[0], m_scr, sem.at[0])]
        copies += [
            pltpu.make_async_copy(
                w.at[pl.ds(at, part)], u_ref.at[pl.ds(n * part, part)], sem.at[1 + n]
            )
            for n, w in enumerate(w_refs)
        ]
        copies += [
            pltpu.make_async_copy(f_ref.at[0, pl.ds(end, LEFT)], near_ref, sem.at[4]),
            pltpu.make_async_copy(f_ref.at[0, pl.ds(top, LEFT)], far_ref, sem.at[5]),
        ]
        for c in copies:
            c.start()
        copies[0].wait()
        folded = [m_scr[:, g * cols : (g + 1) * cols] for g in range(groups)]
        bank_ref[...] = jnp.concatenate(folded, axis=0)
        for c in copies[1:]:
            c.wait()

    hbm = pl.BlockSpec(memory_space=pltpu.HBM)
    vmem = pl.BlockSpec(memory_space=pltpu.VMEM)
    return pl.pallas_call(
        kernel,
        in_specs=[pl.BlockSpec(memory_space=pltpu.SMEM)] + [hbm] * 5,
        out_specs=[vmem] * 4,
        out_shape=[
            jax.ShapeDtypeStruct((3 * part, cols), jnp.bfloat16),
            jax.ShapeDtypeStruct((LEFT, feat), jnp.bfloat16),
            jax.ShapeDtypeStruct((LEFT, feat), jnp.bfloat16),
            jax.ShapeDtypeStruct((groups * segs, cols), jnp.bfloat16),
        ],
        scratch_shapes=[
            pltpu.VMEM((segs, feat), jnp.bfloat16),
            pltpu.SemaphoreType.DMA((6,)),
        ],
        compiler_params=pltpu.CompilerParams(vmem_limit_bytes=4 * MIB),
        name="cut",
    )(ids, *[in_hbm(a) for a in (frames_in, memory_in, *weights)])


def in_hbm(a):
    return pltpu.with_memory_space_constraint(a, pltpu.HBM)


def in_vmem(a):
    return pltpu.with_memory_space_constraint(a, pltpu.VMEM)


def head_lanes(cols, hd):
    return lax.broadcasted_iota(jnp.int32, (1, cols), 1) // hd


def only(a, h, hd):
    return jnp.where(head_lanes(a.shape[1], hd) == h, a, jnp.zeros_like(a))


def split(a):
    return [a[:, j : j + LANES] for j in range(0, a.shape[1], LANES)]


def folded(parts, op):
    out = parts[0]
    for part in parts[1:]:
        out = op(out, part)
    return out


def score_segment(q, k_main, k_tail, hd):
    heads = q.shape[1] // hd
    scale = float(hd) ** (-0.5)
    exact = math.frexp(scale)[0] == 0.5
    if exact:
        q = q * jnp.asarray(scale, q.dtype)
    across = (((1,), (1,)), ((), ()))
    main = lax.dot_general(
        jnp.concatenate([only(q, h, hd) for h in range(heads)], axis=0),
        k_main,
        across,
        preferred_element_type=jnp.float32,
    )
    tail = lax.dot_general(
        q,
        jnp.concatenate([only(k_tail, h, hd) for h in range(heads)], axis=0),
        across,
        preferred_element_type=jnp.float32,
    )
    if not exact:
        main = main * scale
        tail = tail * scale
    return main, tail


def weigh_segment(s_ref, t_ref, p_ref, n_q, heads, tail_n, main_bias, tail_bias):
    main_n = s_ref.shape[1]
    tail_head = lax.broadcasted_iota(jnp.int32, (1, heads * tail_n), 1) // tail_n
    tails = split(t_ref[...] + tail_bias)
    owners = split(tail_head)
    held = [
        [j for j in range(len(tails)) if j * LANES < (h + 1) * tail_n and (j + 1) * LANES > h * tail_n]
        for h in range(heads)
    ]
    tops = []
    sums = []
    for h in range(heads):
        scores = s_ref[h * n_q : (h + 1) * n_q, :] + main_bias
        parts = split(scores) + [jnp.where(owners[j] == h, tails[j], DEAD) for j in held[h]]
        top = jnp.max(folded(parts, jnp.maximum), axis=-1, keepdims=True)
        probs = jnp.exp(scores - top)
        tops.append(top)
        sums.append(folded(split(probs), jnp.add))
        p_ref[:, h * main_n : (h + 1) * main_n] = probs.astype(jnp.bfloat16)
    for j, block in enumerate(tails):
        inside = [h for h in range(heads) if j in held[h]]
        top = tops[inside[0]]
        for h in inside[1:]:
            top = jnp.where(owners[j] >= h, tops[h], top)
        probs = jnp.exp(block - top)
        for h in inside:
            sums[h] = sums[h] + jnp.where(owners[j] == h, probs, 0.0)
        at = heads * main_n + j * LANES
        p_ref[:, at : at + LANES] = probs.astype(jnp.bfloat16)
    return [1.0 / jnp.sum(total, axis=-1, keepdims=True) for total in sums]


def mix_segment(probs, shares, v_main, v_tail, hd):
    heads = v_main.shape[1] // hd
    mixed = jnp.dot(
        probs,
        jnp.concatenate([only(v, h, hd) for v in (v_main, v_tail) for h in range(heads)], axis=0),
        preferred_element_type=jnp.float32,
    )
    outs = []
    for block, head in zip(split(mixed), split(head_lanes(v_main.shape[1], hd))):
        at = len(outs) * LANES
        inside = [h for h in range(heads) if at <= h * hd < at + LANES]
        share = shares[inside[0]]
        for h in inside[1:]:
            share = jnp.where(head >= h, shares[h], share)
        outs.append(block * share)
    return jnp.concatenate(outs, axis=1)


def make_kernel(dims, first, last, sliced, n_buffers, columns, bank_devices, slots):
    utts, rows, feat, cols, segs, seg_len, bank_n = dims
    hd = feat // HEADS
    heads = cols // hd
    main_n = LEFT + seg_len
    tail_n = bank_n + RIGHT
    kv_rows = bank_n + LEFT + rows + RIGHT
    q_base = bank_n + LEFT
    n_slots = len(slots)
    n_before = len(columns) - 1 if last else 0

    def kernel(*refs):
        refs = list(refs)

        def take(n):
            got = refs[:n]
            del refs[:n]
            return got

        ids_ref, len_ref = take(2)
        if first:
            banks = take(2 if sliced else 1)
            _, k_scr, v_scr, q_scr = take(4)
        else:
            (x_ref,) = take(1)
        w_refs = take(n_buffers)
        before = take(n_before)
        if last:
            ctx_ref, mem_ref = take(2)
        else:
            (o_ref,) = take(1)
        if first:
            (x_ref,) = take(1)
        if not first:
            k_scr, v_scr, q_scr = take(3)
        m_scr, s_scr, t_scr, p_scr = take(4)
        k_bank, v_bank = take(2) if first else (k_scr, v_scr)
        if last:
            o_ref, out_sem = take(2)
        seq_index = ids_ref[0]
        odd = seq_index % 2 == 1
        row_base = seq_index * rows
        waits = []

        def column(which):
            kind, value = columns[which]
            index = ids_ref[1] ^ value if kind == "xor" else value
            return pl.multiple_of(index * cols, cols)

        def device(pair):
            return seq_index ^ jnp.where(odd, pair[1], pair[0])

        def write_out(block_ref, at, u, lo, size, target, sem):
            done = pltpu.make_async_copy(
                block_ref.at[u, pl.ds(lo, size)],
                target.at[u, pl.ds(0 if target is mem_ref else lo, size), pl.ds(at, cols)],
                sem,
            )
            done.start()
            waits.append(done)

        for n, block_ref in enumerate(before):
            for u in range(utts):
                write_out(block_ref, column(n), u, 0, rows, ctx_ref, out_sem.at[u, 2 * n])
                write_out(
                    block_ref, column(n), u, rows, segs, mem_ref, out_sem.at[u, 2 * n + 1]
                )

        if first and sliced:
            groups = feat // cols
            blocks = len(bank_devices) // 2
            for n, ref in enumerate(banks):
                top = ref.shape[0] - blocks * groups * segs
                tail = ref[top:, :].astype(jnp.float32)
                for g in range(groups):
                    rows_of = [
                        tail[(b * groups + g) * segs : (b * groups + g + 1) * segs]
                        for b in range(blocks)
                    ]
                    x_ref[
                        0, n * bank_n // 2 : (n + 1) * bank_n // 2, g * cols : (g + 1) * cols
                    ] = jnp.concatenate(rows_of, axis=0).astype(jnp.bfloat16)
        elif first:
            x_ref[:, :bank_n, :] = banks[0][...]

        tail_at = lax.broadcasted_iota(jnp.int32, (1, heads * tail_n), 1) % tail_n
        block = tail_at // segs
        entry = tail_at % segs
        for b, pair in enumerate(bank_devices):
            entry = entry + jnp.where(block == b, device(pair) * segs, 0)
        main_at = lax.broadcasted_iota(jnp.int32, (1, main_n), 1)

        for u in range(utts):
            length = len_ref[u]

            def project(which, lo, hi):
                if first or n_slots == 0:
                    w = w_refs[which - 1][...] if first else w_refs[0][which]
                    return jnp.dot(
                        x_ref[u, lo:hi, :], w, preferred_element_type=jnp.float32
                    ).astype(jnp.bfloat16)
                part = feat // n_slots
                per = n_slots // n_buffers
                acc = None
                for t in range(0, n_slots, 2):
                    lhs = []
                    rhs = []
                    for s in (t, t + 1):
                        at = pl.multiple_of(device(slots[s]) * part, LANES)
                        lhs.append(x_ref[u, lo:hi, pl.ds(at, part)])
                        top = (s % per * 3 + which) * part
                        rhs.append(w_refs[s // per][top : top + part, :])
                    one = jnp.dot(
                        jnp.concatenate(lhs, axis=1),
                        jnp.concatenate(rhs, axis=0),
                        preferred_element_type=jnp.float32,
                    )
                    acc = one if acc is None else acc + one
                return acc.astype(jnp.bfloat16)

            if first:
                k_bank[u] = project(1, 0, bank_n)
                v_bank[u] = project(2, 0, bank_n)
            else:
                k_scr[u] = project(1, 0, kv_rows)
                v_scr[u] = project(2, 0, kv_rows)
                q_scr[u] = project(0, q_base, kv_rows + PAD_ROWS)

            def keys(scr, bank, s):
                win = bank_n + s * seg_len
                edge = win + main_n
                both = [bank[u, :bank_n, :], scr[u, edge : edge + RIGHT, :]]
                return scr[u, win:edge, :], jnp.concatenate(both, axis=0)

            def score(s):
                q = jnp.concatenate(
                    [q_scr[u, s * seg_len : (s + 1) * seg_len, :], q_scr[u, rows + RIGHT :, :]],
                    axis=0,
                )
                s_scr[s % 2], t_scr[s % 2] = score_segment(q, *keys(k_scr, k_bank, s), hd)

            score(0)
            for s in range(segs):
                if s + 1 < segs:
                    score(s + 1)
                seg_index = seq_index * segs + s
                start = row_base + s * seg_len
                main_pos = start - LEFT + main_at
                main_bias = jnp.where((main_pos >= 0) & (main_pos < length), 0.0, DEAD)
                bank_live = (tail_at < bank_n) & (entry < seg_index) & (entry * seg_len < length)
                right_pos = start + seg_len - bank_n + tail_at
                tail_live = bank_live | ((tail_at >= bank_n) & (right_pos < length))
                tail_bias = jnp.where(tail_live, 0.0, DEAD)
                shares = weigh_segment(
                    s_scr.at[s % 2],
                    t_scr.at[s % 2],
                    p_scr.at[s % 2],
                    seg_len + PAD_ROWS,
                    heads,
                    tail_n,
                    main_bias,
                    tail_bias,
                )
                out = mix_segment(p_scr[s % 2], shares, *keys(v_scr, v_bank, s), hd)
                row_at = lax.broadcasted_iota(jnp.int32, (seg_len, 1), 0)
                live = jnp.where(start + row_at < length, out[:seg_len], 0.0)
                o_ref[u, s * seg_len : (s + 1) * seg_len, :] = live.astype(jnp.bfloat16)
                m_scr[u, s : s + 1, :] = out[seg_len + s : seg_len + s + 1]
                if last:
                    write_out(
                        o_ref,
                        column(-1),
                        u,
                        s * seg_len,
                        seg_len,
                        ctx_ref,
                        out_sem.at[u, 2 * n_before + s],
                    )
            o_ref[u, rows : rows + segs, :] = m_scr[u].astype(jnp.bfloat16)
            if last:
                write_out(
                    o_ref, column(-1), u, rows, segs, mem_ref, out_sem.at[u, 2 * n_before + segs]
                )
        for done in waits:
            done.wait()

    return kernel


def prepare(dims, sliced, scalars, frames_in, edges, weights):
    utts, rows, feat, cols, _, seg_len, bank_n = dims
    kv_rows = bank_n + LEFT + rows + RIGHT
    q_base = bank_n + LEFT
    q_rows = rows + RIGHT + PAD_ROWS

    def kernel(ids_ref, len_ref, frames_ref, *refs):
        first_edge, second_edge, wq_ref, wk_ref, wv_ref, x_ref, k_ref, v_ref, q_ref, sem = refs
        seq_index = ids_ref[0]
        odd = seq_index % 2 == 1
        row_base = seq_index * rows
        moves = [
            pltpu.make_async_copy(frames_ref.at[u], x_ref.at[u, pl.ds(q_base, rows)], sem.at[u])
            for u in range(utts)
        ]
        for c in moves:
            c.start()
        if sliced:
            near = first_edge[...]
            far = second_edge[...]
            x_ref[0, bank_n:q_base, :] = jnp.where(odd, near, far)
            x_ref[0, q_base + rows : kv_rows, :] = jnp.where(odd, far[:RIGHT], near[:RIGHT])
        else:
            x_ref[:, bank_n:q_base, :] = first_edge[...]
            x_ref[:, q_base + rows : kv_rows, :] = second_edge[...]
        for c in moves:
            c.wait()
        for u in range(utts):
            length = len_ref[u]
            seg_of = lax.broadcasted_iota(jnp.int32, (PAD_ROWS, rows), 0)
            pos = lax.broadcasted_iota(jnp.int32, (PAD_ROWS, rows), 1)
            pick = (pos // seg_len == seg_of) & (row_base + pos < length)
            sums = jnp.dot(
                jnp.where(pick, 1.0, 0.0).astype(jnp.bfloat16),
                x_ref[u, q_base : q_base + rows, :],
                preferred_element_type=jnp.float32,
            )
            seg = lax.broadcasted_iota(jnp.int32, (PAD_ROWS, 1), 0)
            count = jnp.clip(length - (row_base + seg * seg_len), 1, seg_len)
            mean = sums / count.astype(jnp.float32)
            x_ref[u, kv_rows:, :] = mean.astype(jnp.bfloat16)
            for w_ref, out_ref, lo, hi, at in (
                (wk_ref, k_ref, bank_n, kv_rows, bank_n),
                (wv_ref, v_ref, bank_n, kv_rows, bank_n),
                (wq_ref, q_ref, q_base, kv_rows + PAD_ROWS, 0),
            ):
                out_ref[u, at : at + hi - lo, :] = jnp.dot(
                    x_ref[u, lo:hi, :], w_ref[...], preferred_element_type=jnp.float32
                ).astype(jnp.bfloat16)

    vmem = pl.BlockSpec(memory_space=pltpu.VMEM)
    work = 2 * utts * (2 * kv_rows + q_rows) * feat * cols
    return pl.pallas_call(
        kernel,
        in_specs=[pl.BlockSpec(memory_space=pltpu.SMEM)] * 2
        + [pl.BlockSpec(memory_space=pl.ANY)]
        + [vmem] * 5,
        out_specs=[vmem] * 4,
        out_shape=[
            pltpu.VMEM((utts, kv_rows + PAD_ROWS, feat), jnp.bfloat16),
            pltpu.VMEM((utts, kv_rows, cols), jnp.bfloat16),
            pltpu.VMEM((utts, kv_rows, cols), jnp.bfloat16),
            pltpu.VMEM((utts, q_rows, cols), jnp.bfloat16),
        ],
        scratch_shapes=[pltpu.SemaphoreType.DMA((utts,))],
        compiler_params=pltpu.CompilerParams(vmem_limit_bytes=16 * MIB),
        cost_estimate=pl.CostEstimate(
            flops=4 * work, transcendentals=0, bytes_accessed=utts * kv_rows * feat * 2
        ),
        name="prepare",
    )(*scalars, frames_in, *edges, *weights)


def attend_chunk(
    dims, sliced, first, last, scalars, inputs, weights, columns, bank_devices, slots, before=()
):
    utts, rows, feat, cols, segs, seg_len, bank_n = dims
    kv_rows = bank_n + LEFT + rows + RIGHT
    q_rows = rows + RIGHT + PAD_ROWS
    block = (utts, rows + PAD_ROWS, cols)
    anywhere = pl.BlockSpec(memory_space=pl.ANY)
    vmem = pl.BlockSpec(memory_space=pltpu.VMEM)
    smem = pl.BlockSpec(memory_space=pltpu.SMEM)
    held = [in_vmem(x) for x in (inputs[-4:] if first else inputs)]
    inputs = [*inputs[:-4], *held] if first else held
    before = [in_vmem(b) for b in before]
    args = [*scalars, *inputs, *weights, *before]
    heads = cols * HEADS // feat
    n_q = seg_len + PAD_ROWS
    main_n = LEFT + seg_len
    tail_n = bank_n + RIGHT
    scratch = [
        pltpu.VMEM((utts, segs, cols), jnp.float32),
        pltpu.VMEM((2, heads * n_q, main_n), jnp.float32),
        pltpu.VMEM((2, n_q, heads * tail_n), jnp.float32),
        pltpu.VMEM((2, n_q, heads * (main_n + tail_n)), jnp.bfloat16),
    ]
    if first:
        scratch += [pltpu.VMEM((utts, bank_n, cols), jnp.bfloat16)] * 2
    else:
        scratch = [
            pltpu.VMEM((utts, kv_rows, cols), jnp.bfloat16),
            pltpu.VMEM((utts, kv_rows, cols), jnp.bfloat16),
            pltpu.VMEM((utts, q_rows, cols), jnp.bfloat16),
        ] + scratch
    in_specs = [smem] * 2 + [vmem] * (len(inputs) + len(weights))
    in_specs += [vmem] * len(before)
    aliases = {}
    if last:
        out_specs = [anywhere] * 2
        out_shape = [
            jax.ShapeDtypeStruct((utts, rows, feat), jnp.bfloat16),
            jax.ShapeDtypeStruct((utts, segs, feat), jnp.bfloat16),
        ]
        scratch += [
            pltpu.VMEM(block, jnp.bfloat16),
            pltpu.SemaphoreType.DMA((utts, 2 * len(before) + segs + 1)),
        ]
    else:
        out_specs = [vmem]
        out_shape = [pltpu.VMEM(block, jnp.bfloat16)]
    if first:
        out_specs.append(vmem)
        out_shape.append(pltpu.VMEM((utts, kv_rows + PAD_ROWS, feat), jnp.bfloat16))
        aliases = {2 + len(inputs) - 4: 1}
    work = 2 * utts * (2 * kv_rows + q_rows) * feat * cols
    return pl.pallas_call(
        make_kernel(dims, first, last, sliced, len(weights), columns, bank_devices, slots),
        in_specs=in_specs,
        out_specs=out_specs,
        out_shape=out_shape,
        scratch_shapes=scratch,
        input_output_aliases=aliases,
        compiler_params=pltpu.CompilerParams(vmem_limit_bytes=16 * MIB),
        cost_estimate=pl.CostEstimate(
            flops=4 * work, transcendentals=0, bytes_accessed=utts * kv_rows * feat * 2
        ),
        name="attend_first" if first else "attend_next",
    )(*args)


def local(frames_in, memory_in, w_query, w_key, w_value, lengths):
    utts, rows, feat = frames_in.shape
    segs = memory_in.shape[1]
    seg_len = rows // segs
    seq_count = lax.axis_size("seq")
    dp_count = lax.axis_size("dp")
    ids = jnp.stack([lax.axis_index("seq"), lax.axis_index("dp")]).astype(jnp.int32)
    bank_n = segs * seq_count
    part = feat // seq_count
    weights = (w_query, w_key, w_value)
    width = w_query.shape[1]
    sliced = (
        utts == 1
        and len(stage_masks(seq_count)) == 3
        and dp_count & (dp_count - 1) == 0
        and part % LANES == 0
        and width % LANES == 0
        and feat // width * segs % PAD_ROWS == 0
        and 4 * segs % PAD_ROWS == 0
        and RIGHT <= LEFT <= rows
    )
    cols = width if sliced else feat // 4
    dims = (utts, rows, feat, cols, segs, seg_len, bank_n)

    if sliced:
        mine, near_sent, far_sent, own_bank = cut(ids, part, frames_in, memory_in, weights)
        arrived = {0: mine}
        arrived[1] = swapped(mine, "dp", (1, 1))
        pair_bank = [own_bank, swapped(own_bank, "seq", (1, 1))]
        near = swapped(near_sent, "seq", (1, 1))
        inner = [(i, i + 1) for i in range(1, seq_count - 1, 2)]
        far = lax.ppermute(far_sent, "seq", inner + [(b, a) for a, b in inner])
        for r in range(2, dp_count):
            low = r & -r
            arrived[r] = swapped(arrived[r ^ low], "dp", (low, low))
        later = []
        firsts = {}
        for r in range(1, dp_count):
            low = r & -r
            if r != low:
                firsts[r] = swapped(firsts[r ^ low], "dp", (low, low))
            buffers, slots, firsts[r] = gather_slices(
                arrived[r], "seq", pair_bank if r == 1 else None, firsts.get(r)
            )
            later.append((("xor", r), slots, buffers))
        own = (("xor", 0), weights)
        edges = (near, far)
        banks = tuple(later[0][2][:2])
        bank_devices = [(e ^ h, o ^ h) for e, o in later[0][1][:4] for h in (0, 1)]
    else:
        full = [lax.all_gather(w, "dp", axis=1, tiled=True) for w in weights]
        chunks = [
            (("at", c), [w[:, c * cols : (c + 1) * cols] for w in full]) for c in range(feat // cols)
        ]
        own = chunks[0]
        later = [(c, [], [jnp.stack(ws)]) for c, ws in chunks[1:]]
        left = shifted(frames_in[:, rows - LEFT :], "seq", 1)
        right = shifted(frames_in[:, :RIGHT], "seq", -1)
        edges = (left, right)
        banks = (gather_bank(memory_in, "seq"),)
        bank_devices = [(t, t) for t in range(seq_count)]

    scalars = (ids, lengths)
    prepared = prepare(dims, sliced, scalars, frames_in, edges, own[1])
    block, x_all = attend_chunk(
        dims,
        sliced,
        True,
        False,
        scalars,
        (*banks, *prepared),
        own[1][1:],
        [own[0]],
        bank_devices,
        [],
    )
    blocks = [block]
    columns = [own[0]]
    for n, (source, slots, buffers) in enumerate(later):
        last = n == len(later) - 1
        columns.append(source)
        outs = attend_chunk(
            dims,
            sliced,
            False,
            last,
            scalars,
            (x_all,),
            buffers,
            list(columns),
            bank_devices,
            slots,
            blocks if last else (),
        )
        blocks.append(outs[0])
    return tuple(outs)


def solution(mesh):
    placed = (
        P("dp", "seq", None),
        P("dp", "seq", None),
        P(None, "dp"),
        P(None, "dp"),
        P(None, "dp"),
        P("dp"),
    )
    return jax.shard_map(
        local,
        mesh=mesh,
        in_specs=placed,
        out_specs=(P("dp", "seq", None), P("dp", "seq", None)),
        check_vma=False,
    )
```

profile of v0, /device:TPU:3, one launch (start us, length us, event | category | flops | bytes accessed | tf_op | source)
XLA Modules:
  0.0 57.1 jit_solution(15376968494356178352)
XLA Ops:
  0.6 0.1 pad_add_fusion.ids_ref.refs_0_
  0.7 1.7 %cut.1 = (bf16[384,256]{1,0:T(8,128)(2,1)S(1)}, bf16[128,1024]{1,0:T(8,128)(2,1)S(1)}, bf16[128,1024]{1,0:T(8,128)(2,1)S(1)}, bf16[16,256]{1,0:T(8,128)(2,1)S(1)}) custom-call(s32[2]{0:T(128)S(1)} %pad_add_fusion.ids_ref.refs_0_, bf16[1,512,1024]{2,1,0:T(8,128)(2,1)} %frames_ref.1, bf16[1,4,1024]{2,1,0:T(4,128)(2,1)} %m_ref.1, bf16[1024,256]{1,0:T(8,128)(2,1)} %refs_2_.3, ...), custom_call_target="tpu_custom_call" | custom-call | tf_op jit(solution)/shard_map/cut/pallas_call | solution.py:107
  2.5 1.4 %collective-permute-start = (bf16[384,256]{1,0:T(8,128)(2,1)S(1)}, bf16[384,256]{1,0:T(8,128)(2,1)S(1)}, u32[]{:S(2)}, u32[]{:S(2)}) collective-permute-start(bf16[384,256]{1,0:T(8,128)(2,1)S(1)} %get-tuple-element.12), channel_id=1, source_target_pairs={{0,8},{8,0},{16,24},{24,16},{1,9},{9,1},{17,25},{25,17},{2,10},{10... | collective-permute-start | bytes 589832 | tf_op jit(solution)/shard_map/ppermute | solution.py:28
  3.8 2.3 %collective-permute-start.6 = (bf16[384,256]{1,0:T(8,128)(2,1)S(1)}, bf16[384,256]{1,0:T(8,128)(2,1)S(1)}, u32[]{:S(2)}, u32[]{:S(2)}) collective-permute-start(bf16[384,256]{1,0:T(8,128)(2,1)S(1)} %get-tuple-element.12), channel_id=1, source_target_pairs={{0,16},{8,24},{16,0},{24,8},{1,17},{9,25},{17,1},{25,9},{2,18},{10... | collective-permute-start | bytes 589832 | tf_op jit(solution)/shard_map/ppermute | solution.py:28
  6.1 1.2 %collective-permute-start.1 = (bf16[16,256]{1,0:T(8,128)(2,1)S(1)}, bf16[16,256]{1,0:T(8,128)(2,1)S(1)}, u32[]{:S(2)}, u32[]{:S(2)}) collective-permute-start(bf16[16,256]{1,0:T(8,128)(2,1)S(1)} %get-tuple-element.13), channel_id=1, source_target_pairs={{0,1},{1,0},{2,3},{3,2},{4,5},{5,4},{6,7},{7,6},{8,9},{9,8},{10,11... | collective-permute-start | bytes 24584 | tf_op jit(solution)/shard_map/ppermute | solution.py:28
  7.4 3.5 %collective-permute-start.5 = (bf16[128,1024]{1,0:T(8,128)(2,1)S(1)}, bf16[128,1024]{1,0:T(8,128)(2,1)S(1)}, u32[]{:S(2)}, u32[]{:S(2)}) collective-permute-start(bf16[128,1024]{1,0:T(8,128)(2,1)S(1)} %get-tuple-element.15), channel_id=1, source_target_pairs={{1,2},{3,4},{5,6},{2,1},{4,3},{6,5},{9,10},{11,12},{13,14},{10,9},... | collective-permute-start | bytes 786440 | tf_op jit(solution)/shard_map/ppermute | solution.py:589
  11.6 0.4 collective-permute-done
  12.1 1.3 %collective-permute-start.8 = (bf16[384,256]{1,0:T(8,128)(2,1)S(1)}, bf16[384,256]{1,0:T(8,128)(2,1)S(1)}, u32[]{:S(2)}, u32[]{:S(2)}) collective-permute-start(bf16[384,256]{1,0:T(8,128)(2,1)S(1)} %collective-permute-done.6), channel_id=1, source_target_pairs={{0,2},{1,5},{2,0},{3,7},{4,6},{5,1},{6,4},{7,3},{8,10},{9,13},{10,... | collective-permute-start | bytes 589832 | tf_op jit(solution)/shard_map/ppermute | solution.py:28
  13.4 0.2 collective-permute-start.2
  13.6 2.8 %collective-permute-start.7 = (bf16[384,256]{1,0:T(8,128)(2,1)S(1)}, bf16[384,256]{1,0:T(8,128)(2,1)S(1)}, u32[]{:S(2)}, u32[]{:S(2)}) collective-permute-start(bf16[384,256]{1,0:T(8,128)(2,1)S(1)} %collective-permute-done.6), channel_id=1, source_target_pairs={{0,8},{8,0},{16,24},{24,16},{1,9},{9,1},{17,25},{25,17},{2,10},{10... | collective-permute-start | bytes 589832 | tf_op jit(solution)/shard_map/ppermute | solution.py:28
  16.5 2.3 %collective-permute-done.8 = bf16[384,256]{1,0:T(8,128)(2,1)S(1)} collective-permute-done((bf16[384,256]{1,0:T(8,128)(2,1)S(1)}, bf16[384,256]{1,0:T(8,128)(2,1)S(1)}, u32[]{:S(2)}, u32[]{:S(2)}) %collective-permute-start.8) | collective-permute-done | bytes 196640 | tf_op jit(solution)/shard_map/ppermute | solution.py:28
  18.8 1.0 %collective-permute-done.7 = bf16[384,256]{1,0:T(8,128)(2,1)S(1)} collective-permute-done((bf16[384,256]{1,0:T(8,128)(2,1)S(1)}, bf16[384,256]{1,0:T(8,128)(2,1)S(1)}, u32[]{:S(2)}, u32[]{:S(2)}) %collective-permute-start.7) | collective-permute-done | bytes 196640 | tf_op jit(solution)/shard_map/ppermute | solution.py:28
  19.8 5.1 %collective-permute-start.16 = (bf16[768,256]{1,0:T(8,128)(2,1)S(1)}, bf16[768,256]{1,0:T(8,128)(2,1)S(1)}, u32[]{:S(2)}, u32[]{:S(2)}) collective-permute-start(bf16[768,256]{1,0:T(8,128)(2,1)S(1)} %constant_dynamic-update-slice_fusion.2.refs_3_), channel_id=1, source_target_pairs={{0,1},{1,0},{2,3},{3,2},{4,5},{5,4},{6,7},{7,6},{8,9},{9,8},{10,11... | collective-permute-start | bytes 1179656 | tf_op jit(solution)/shard_map/ppermute | solution.py:28
  25.1 4.8 %collective-permute-done.9 = bf16[384,256]{1,0:T(8,128)(2,1)S(1)} collective-permute-done((bf16[384,256]{1,0:T(8,128)(2,1)S(1)}, bf16[384,256]{1,0:T(8,128)(2,1)S(1)}, u32[]{:S(2)}, u32[]{:S(2)}) %collective-permute-start.9) | collective-permute-done | bytes 196640 | tf_op jit(solution)/shard_map/ppermute | solution.py:28
  29.9 1.5 %collective-permute-start.10 = (bf16[768,256]{1,0:T(8,128)(2,1)S(1)}, bf16[768,256]{1,0:T(8,128)(2,1)S(1)}, u32[]{:S(2)}, u32[]{:S(2)}) collective-permute-start(bf16[768,256]{1,0:T(8,128)(2,1)S(1)} %constant_dynamic-update-slice_fusion.refs_3_), channel_id=1, source_target_pairs={{0,4},{1,3},{2,6},{3,1},{4,0},{5,7},{6,2},{7,5},{8,12},{9,11},{10,... | collective-permute-start | bytes 1179656 | tf_op jit(solution)/shard_map/ppermute | solution.py:28
  31.4 3.8 %collective-permute-start.17 = (bf16[768,256]{1,0:T(8,128)(2,1)S(1)}, bf16[768,256]{1,0:T(8,128)(2,1)S(1)}, u32[]{:S(2)}, u32[]{:S(2)}) collective-permute-start(bf16[768,256]{1,0:T(8,128)(2,1)S(1)} %collective-permute-done.15.refs_4_), channel_id=1, source_target_pairs={{0,1},{1,0},{2,3},{3,2},{4,5},{5,4},{6,7},{7,6},{8,9},{9,8},{10,11... | collective-permute-start | bytes 1179656 | tf_op jit(solution)/shard_map/ppermute | solution.py:28
  35.3 2.0 %prepare.1 = (bf16[1,720,1024]{2,1,0:T(8,128)(2,1)S(1)}, bf16[1,704,256]{2,1,0:T(8,128)(2,1)S(1)}, bf16[1,704,256]{2,1,0:T(8,128)(2,1)S(1)}, bf16[1,560,256]{2,1,0:T(8,128)(2,1)S(1)}) custom-call(s32[2]{0:T(128)S(1)} %pad_add_fusion.ids_ref.refs_0_, s32[1]{0:T(128)S(6)} %copy.18.len_ref.refs_1_, bf16[1,512,1024]{2,1,0:T(8,128)(2,1)S(1)} %copy-done, ...), custom_call_target="tpu_custom_call" | custom-call | flops 4127195136 | bytes 1441792 | tf_op jit(solution)/shard_map/prepare/pallas_call | solution.py:469
  37.3 0.1 collective-permute-start.13
  37.4 3.8 %collective-permute-start.14 = (bf16[832,256]{1,0:T(8,128)(2,1)S(1)}, bf16[832,256]{1,0:T(8,128)(2,1)S(1)}, u32[]{:S(2)}, u32[]{:S(2)}) collective-permute-start(bf16[832,256]{1,0:T(8,128)(2,1)S(1)} %collective-permute-done.3.refs_3_.refs_4_), channel_id=1, source_target_pairs={{0,1},{1,0},{2,3},{3,2},{4,5},{5,4},{6,7},{7,6},{8,9},{9,8},{10,11... | collective-permute-start | bytes 1277960 | tf_op jit(solution)/shard_map/ppermute | solution.py:28
  41.2 2.4 %attend_first.1 = (bf16[1,528,256]{2,1,0:T(8,128)(2,1)S(1)}, bf16[1,720,1024]{2,1,0:T(8,128)(2,1)S(1)}) custom-call(s32[2]{0:T(128)S(1)} %pad_add_fusion.ids_ref.refs_0_, s32[1]{0:T(128)S(6)} %copy.18.len_ref.refs_1_, bf16[832,256]{1,0:T(8,128)(2,1)S(1)} %slice_dynamic-update-slice_fusion.1.refs_2_.refs_3_, ...), custom_call_target="tpu_custom_call", output_to_operand_aliasing={{1}: (4, {})} | custom-call | flops 4127195136 | bytes 1441792 | tf_op jit(solution)/shard_map/attend_first/pallas_call | solution.py:543
  43.6 1.7 %collective-permute-start.12 = (bf16[768,256]{1,0:T(8,128)(2,1)S(1)}, bf16[768,256]{1,0:T(8,128)(2,1)S(1)}, u32[]{:S(2)}, u32[]{:S(2)}) collective-permute-start(bf16[768,256]{1,0:T(8,128)(2,1)S(1)} %collective-permute-done.10.refs_4_), channel_id=1, source_target_pairs={{0,1},{1,0},{2,3},{3,2},{4,5},{5,4},{6,7},{7,6},{8,9},{9,8},{10,11... | collective-permute-start | bytes 1179656 | tf_op jit(solution)/shard_map/ppermute | solution.py:28
  45.4 3.6 %attend_next.4.refs_9_ = bf16[1,528,256]{2,1,0:T(8,128)(2,1)S(1)} custom-call(s32[2]{0:T(128)S(1)} %pad_add_fusion.ids_ref.refs_0_, s32[1]{0:T(128)S(6)} %copy.18.len_ref.refs_1_, bf16[1,720,1024]{2,1,0:T(8,128)(2,1)S(1)} %get-tuple-element.20.refs_2_, bf16[768,256]{1,0:T(8,128)(2,1)S(1)} %constant_dynamic-update-slice_fusion.2.refs_3_, ...), custom_call_target="tpu_custom_call" | custom-call | flops 4127195136 | bytes 1441792 | tf_op jit(solution)/shard_map/attend_next/pallas_call | solution.py:543
  49.0 3.6 %attend_next.3.refs_8_ = bf16[1,528,256]{2,1,0:T(8,128)(2,1)S(1)} custom-call(s32[2]{0:T(128)S(1)} %pad_add_fusion.ids_ref.refs_0_, s32[1]{0:T(128)S(6)} %copy.18.len_ref.refs_1_, bf16[1,720,1024]{2,1,0:T(8,128)(2,1)S(1)} %get-tuple-element.20.refs_2_, bf16[832,256]{1,0:T(8,128)(2,1)S(1)} %slice_dynamic-update-slice_fusion.1.refs_2_.refs_3_, ...), custom_call_target="tpu_custom_call" | custom-call | flops 4127195136 | bytes 1441792 | tf_op jit(solution)/shard_map/attend_next/pallas_call | solution.py:543
  52.7 4.4 %attend_next.5 = (bf16[1,512,1024]{2,1,0:T(8,128)(2,1)}, bf16[1,4,1024]{2,1,0:T(4,128)(2,1)}) custom-call(s32[2]{0:T(128)S(1)} %pad_add_fusion.ids_ref.refs_0_, s32[1]{0:T(128)S(6)} %copy.18.len_ref.refs_1_, bf16[1,720,1024]{2,1,0:T(8,128)(2,1)S(1)} %get-tuple-element.20.refs_2_, bf16[768,256]{1,0:T(8,128)(2,1)S(1)} %constant_dynamic-update-slice_fusion.refs_3_, ...), custom_call_target="tpu_custom_call" | custom-call | flops 4127195136 | bytes 1441792 | tf_op jit(solution)/shard_map/attend_next/pallas_call | solution.py:543
  (39 shorter events, 0.4 us)
Async XLA Ops:
  2.5 9.5 %collective-permute-start = (bf16[384,256]{1,0:T(8,128)(2,1)S(1)}, bf16[384,256]{1,0:T(8,128)(2,1)S(1)}, u32[]{:S(2)}, u32[]{:S(2)}) collective-permute-start(bf16[384,256]{1,0:T(8,128)(2,1)S(1)} %get-tuple-element.12), channel_id=1, source_target_pairs={{0,8},{8,0},{16,24},{24,16},{1,9},{9,1},{17,25},{25,17},{2,10},{10... | collective-permute-start | bytes 589832 | tf_op jit(solution)/shard_map/ppermute | solution.py:28
  3.8 8.2 %collective-permute-start.6 = (bf16[384,256]{1,0:T(8,128)(2,1)S(1)}, bf16[384,256]{1,0:T(8,128)(2,1)S(1)}, u32[]{:S(2)}, u32[]{:S(2)}) collective-permute-start(bf16[384,256]{1,0:T(8,128)(2,1)S(1)} %get-tuple-element.12), channel_id=1, source_target_pairs={{0,16},{8,24},{16,0},{24,8},{1,17},{9,25},{17,1},{25,9},{2,18},{10... | collective-permute-start | bytes 589832 | tf_op jit(solution)/shard_map/ppermute | solution.py:28
  6.1 7.2 %collective-permute-start.1 = (bf16[16,256]{1,0:T(8,128)(2,1)S(1)}, bf16[16,256]{1,0:T(8,128)(2,1)S(1)}, u32[]{:S(2)}, u32[]{:S(2)}) collective-permute-start(bf16[16,256]{1,0:T(8,128)(2,1)S(1)} %get-tuple-element.13), channel_id=1, source_target_pairs={{0,1},{1,0},{2,3},{3,2},{4,5},{5,4},{6,7},{7,6},{8,9},{9,8},{10,11... | collective-permute-start | bytes 24584 | tf_op jit(solution)/shard_map/ppermute | solution.py:28
  7.4 22.5 %collective-permute-start.4 = (bf16[128,1024]{1,0:T(8,128)(2,1)S(1)}, bf16[128,1024]{1,0:T(8,128)(2,1)S(1)}, u32[]{:S(2)}, u32[]{:S(2)}) collective-permute-start(bf16[128,1024]{1,0:T(8,128)(2,1)S(1)} %get-tuple-element.14), channel_id=1, source_target_pairs={{0,1},{1,0},{2,3},{3,2},{4,5},{5,4},{6,7},{7,6},{8,9},{9,8},{10,11... | collective-permute-start | bytes 786440 | tf_op jit(solution)/shard_map/ppermute | solution.py:28
  7.4 27.9 %collective-permute-start.5 = (bf16[128,1024]{1,0:T(8,128)(2,1)S(1)}, bf16[128,1024]{1,0:T(8,128)(2,1)S(1)}, u32[]{:S(2)}, u32[]{:S(2)}) collective-permute-start(bf16[128,1024]{1,0:T(8,128)(2,1)S(1)} %get-tuple-element.15), channel_id=1, source_target_pairs={{1,2},{3,4},{5,6},{2,1},{4,3},{6,5},{9,10},{11,12},{13,14},{10,9},... | collective-permute-start | bytes 786440 | tf_op jit(solution)/shard_map/ppermute | solution.py:589
  11.5 23.7 %copy-start = (bf16[1,512,1024]{2,1,0:T(8,128)(2,1)S(1)}, bf16[1,512,1024]{2,1,0:T(8,128)(2,1)}, u32[]{:S(2)}) copy-start(bf16[1,512,1024]{2,1,0:T(8,128)(2,1)} %frames_ref.1) | copy-start | bytes 3145732
  11.5 23.7 %copy-start.1 = (bf16[1024,256]{1,0:T(8,128)(2,1)S(1)}, bf16[1024,256]{1,0:T(8,128)(2,1)}, u32[]{:S(2)}) copy-start(bf16[1024,256]{1,0:T(8,128)(2,1)} %refs_2_.3) | copy-start | bytes 1572868
  11.6 23.7 %copy-start.2 = (bf16[1024,256]{1,0:T(8,128)(2,1)S(1)}, bf16[1024,256]{1,0:T(8,128)(2,1)}, u32[]{:S(2)}) copy-start(bf16[1024,256]{1,0:T(8,128)(2,1)} %refs_8_.1) | copy-start | bytes 1572868
  11.6 23.7 %copy-start.3 = (bf16[1024,256]{1,0:T(8,128)(2,1)S(1)}, bf16[1024,256]{1,0:T(8,128)(2,1)}, u32[]{:S(2)}) copy-start(bf16[1024,256]{1,0:T(8,128)(2,1)} %refs_9_.1) | copy-start | bytes 1572868
  12.1 6.7 %collective-permute-start.8 = (bf16[384,256]{1,0:T(8,128)(2,1)S(1)}, bf16[384,256]{1,0:T(8,128)(2,1)S(1)}, u32[]{:S(2)}, u32[]{:S(2)}) collective-permute-start(bf16[384,256]{1,0:T(8,128)(2,1)S(1)} %collective-permute-done.6), channel_id=1, source_target_pairs={{0,2},{1,5},{2,0},{3,7},{4,6},{5,1},{6,4},{7,3},{8,10},{9,13},{10,... | collective-permute-start | bytes 589832 | tf_op jit(solution)/shard_map/ppermute | solution.py:28
  13.4 11.6 %collective-permute-start.2 = (bf16[416,256]{1,0:T(8,128)(2,1)S(1)}, bf16[416,256]{1,0:T(8,128)(2,1)S(1)}, u32[]{:S(2)}, u32[]{:S(2)}) collective-permute-start(bf16[416,256]{1,0:T(8,128)(2,1)S(1)} %constant_dynamic-update-slice_fusion.6), channel_id=1, source_target_pairs={{0,2},{1,5},{2,0},{3,7},{4,6},{5,1},{6,4},{7,3},{8,10},{9,13},{10,... | collective-permute-start | bytes 638984 | tf_op jit(solution)/shard_map/ppermute | solution.py:28
  13.6 6.2 %collective-permute-start.7 = (bf16[384,256]{1,0:T(8,128)(2,1)S(1)}, bf16[384,256]{1,0:T(8,128)(2,1)S(1)}, u32[]{:S(2)}, u32[]{:S(2)}) collective-permute-start(bf16[384,256]{1,0:T(8,128)(2,1)S(1)} %collective-permute-done.6), channel_id=1, source_target_pairs={{0,8},{8,0},{16,24},{24,16},{1,9},{9,1},{17,25},{25,17},{2,10},{10... | collective-permute-start | bytes 589832 | tf_op jit(solution)/shard_map/ppermute | solution.py:28
  18.8 12.7 %collective-permute-start.15 = (bf16[768,256]{1,0:T(8,128)(2,1)S(1)}, bf16[768,256]{1,0:T(8,128)(2,1)S(1)}, u32[]{:S(2)}, u32[]{:S(2)}) collective-permute-start(bf16[768,256]{1,0:T(8,128)(2,1)S(1)} %constant_dynamic-update-slice_fusion.2.refs_3_), channel_id=1, source_target_pairs={{0,4},{1,3},{2,6},{3,1},{4,0},{5,7},{6,2},{7,5},{8,12},{9,11},{10,... | collective-permute-start | bytes 1179656 | tf_op jit(solution)/shard_map/ppermute | solution.py:28
  19.8 23.7 %collective-permute-start.16 = (bf16[768,256]{1,0:T(8,128)(2,1)S(1)}, bf16[768,256]{1,0:T(8,128)(2,1)S(1)}, u32[]{:S(2)}, u32[]{:S(2)}) collective-permute-start(bf16[768,256]{1,0:T(8,128)(2,1)S(1)} %constant_dynamic-update-slice_fusion.2.refs_3_), channel_id=1, source_target_pairs={{0,1},{1,0},{2,3},{3,2},{4,5},{5,4},{6,7},{7,6},{8,9},{9,8},{10,11... | collective-permute-start | bytes 1179656 | tf_op jit(solution)/shard_map/ppermute | solution.py:28
  24.9 5.0 %collective-permute-start.9 = (bf16[384,256]{1,0:T(8,128)(2,1)S(1)}, bf16[384,256]{1,0:T(8,128)(2,1)S(1)}, u32[]{:S(2)}, u32[]{:S(2)}) collective-permute-start(bf16[384,256]{1,0:T(8,128)(2,1)S(1)} %collective-permute-done.8), channel_id=1, source_target_pairs={{0,8},{8,0},{16,24},{24,16},{1,9},{9,1},{17,25},{25,17},{2,10},{10... | collective-permute-start | bytes 589832 | tf_op jit(solution)/shard_map/ppermute | solution.py:28
  29.9 7.5 %collective-permute-start.3 = (bf16[832,256]{1,0:T(8,128)(2,1)S(1)}, bf16[832,256]{1,0:T(8,128)(2,1)S(1)}, u32[]{:S(2)}, u32[]{:S(2)}) collective-permute-start(bf16[832,256]{1,0:T(8,128)(2,1)S(1)} %slice_dynamic-update-slice_fusion.1.refs_2_.refs_3_), channel_id=1, source_target_pairs={{0,4},{1,3},{2,6},{3,1},{4,0},{5,7},{6,2},{7,5},{8,12},{9,11},{10,... | collective-permute-start | bytes 1277960 | tf_op jit(solution)/shard_map/ppermute | solution.py:28
  29.9 13.7 %collective-permute-start.10 = (bf16[768,256]{1,0:T(8,128)(2,1)S(1)}, bf16[768,256]{1,0:T(8,128)(2,1)S(1)}, u32[]{:S(2)}, u32[]{:S(2)}) collective-permute-start(bf16[768,256]{1,0:T(8,128)(2,1)S(1)} %constant_dynamic-update-slice_fusion.refs_3_), channel_id=1, source_target_pairs={{0,4},{1,3},{2,6},{3,1},{4,0},{5,7},{6,2},{7,5},{8,12},{9,11},{10,... | collective-permute-start | bytes 1179656 | tf_op jit(solution)/shard_map/ppermute | solution.py:28
  31.4 13.9 %collective-permute-start.17 = (bf16[768,256]{1,0:T(8,128)(2,1)S(1)}, bf16[768,256]{1,0:T(8,128)(2,1)S(1)}, u32[]{:S(2)}, u32[]{:S(2)}) collective-permute-start(bf16[768,256]{1,0:T(8,128)(2,1)S(1)} %collective-permute-done.15.refs_4_), channel_id=1, source_target_pairs={{0,1},{1,0},{2,3},{3,2},{4,5},{5,4},{6,7},{7,6},{8,9},{9,8},{10,11... | collective-permute-start | bytes 1179656 | tf_op jit(solution)/shard_map/ppermute | solution.py:28
  37.3 11.7 %collective-permute-start.13 = (bf16[832,256]{1,0:T(8,128)(2,1)S(1)}, bf16[832,256]{1,0:T(8,128)(2,1)S(1)}, u32[]{:S(2)}, u32[]{:S(2)}) collective-permute-start(bf16[832,256]{1,0:T(8,128)(2,1)S(1)} %slice_dynamic-update-slice_fusion.1.refs_2_.refs_3_), channel_id=1, source_target_pairs={{0,1},{1,0},{2,3},{3,2},{4,5},{5,4},{6,7},{7,6},{8,9},{9,8},{10,11... | collective-permute-start | bytes 1277960 | tf_op jit(solution)/shard_map/ppermute | solution.py:28
  37.4 11.6 %collective-permute-start.14 = (bf16[832,256]{1,0:T(8,128)(2,1)S(1)}, bf16[832,256]{1,0:T(8,128)(2,1)S(1)}, u32[]{:S(2)}, u32[]{:S(2)}) collective-permute-start(bf16[832,256]{1,0:T(8,128)(2,1)S(1)} %collective-permute-done.3.refs_3_.refs_4_), channel_id=1, source_target_pairs={{0,1},{1,0},{2,3},{3,2},{4,5},{5,4},{6,7},{7,6},{8,9},{9,8},{10,11... | collective-permute-start | bytes 1277960 | tf_op jit(solution)/shard_map/ppermute | solution.py:28
  43.5 9.1 %collective-permute-start.11 = (bf16[768,256]{1,0:T(8,128)(2,1)S(1)}, bf16[768,256]{1,0:T(8,128)(2,1)S(1)}, u32[]{:S(2)}, u32[]{:S(2)}) collective-permute-start(bf16[768,256]{1,0:T(8,128)(2,1)S(1)} %constant_dynamic-update-slice_fusion.refs_3_), channel_id=1, source_target_pairs={{0,1},{1,0},{2,3},{3,2},{4,5},{5,4},{6,7},{7,6},{8,9},{9,8},{10,11... | collective-permute-start | bytes 1179656 | tf_op jit(solution)/shard_map/ppermute | solution.py:28
  43.6 9.0 %collective-permute-start.12 = (bf16[768,256]{1,0:T(8,128)(2,1)S(1)}, bf16[768,256]{1,0:T(8,128)(2,1)S(1)}, u32[]{:S(2)}, u32[]{:S(2)}) collective-permute-start(bf16[768,256]{1,0:T(8,128)(2,1)S(1)} %collective-permute-done.10.refs_4_), channel_id=1, source_target_pairs={{0,1},{1,0},{2,3},{3,2},{4,5},{5,4},{6,7},{7,6},{8,9},{9,8},{10,11... | collective-permute-start | bytes 1179656 | tf_op jit(solution)/shard_map/ppermute | solution.py:28
where the time goes:
time: 57.8 us; the launch traced here: 57.1 us
  starting transfers between devices  29 us (50%)
  Pallas kernels  17.7 us (31%)
  waiting for transfers between devices  8.53 us (15%)
  between operations  1.54 us (3%)
    ppermute x17, starting transfers between devices, swapped(): lax.ppermute(block, axis, [(i, i ^ masks[i % 2]) for i in range(count)])  25.5 us
    pallas_call x4, Pallas kernels, attend_chunk(): pl.pallas_call(make_kernel(dims, first, last, sliced, len(weights), colum...  14 us
    ppermute x17, waiting for transfers between devices, swapped(): lax.ppermute(block, axis, [(i, i ^ masks[i % 2]) for i in range(count)])  8.53 us
    ppermute x1, starting transfers between devices, local(): far = lax.ppermute(far_sent, 'seq', inner + [(b, a) for a, b in inner])  3.5 us
    pallas_call x1, Pallas kernels, prepare(): pl.pallas_call(kernel, in_specs=[pl.BlockSpec(memory_space=pltpu.SMEM)] *...  1.99 us
    pallas_call x1, Pallas kernels, cut(): pl.pallas_call(kernel, in_specs=[pl.BlockSpec(memory_space=pltpu.SMEM)] +...  1.75 us
  transfers between devices with their start and end apart: 18, of which 4 were waited for; matrix products, arithmetic and copies ran while one was open for 0% of the time, Pallas kernels for 20%

commit v1 on v0

--- a/solution.py
+++ b/solution.py
@@ -47,6 +47,15 @@
 def gather_slices(mine, axis, tail=None, got=None):
     (even_a, odd_a), (even_b, odd_b) = stage_masks(lax.axis_size(axis))[:2]
     size = mine.shape[0]
+    if got is not None:
+        blocks = [mine, got]
+        for n in range(2):
+            blocks.append(swapped(blocks[n], axis, (even_b, odd_b)))
+        for n in range(4):
+            blocks.append(swapped(blocks[n], axis, (1, 1)))
+        slots = [(0, 0), (even_a, odd_a), (even_b, odd_b), (even_a ^ even_b, odd_a ^ odd_b)]
+        slots += [(o ^ 1, e ^ 1) for e, o in slots]
+        return blocks, slots, got
     sent = mine if tail is None else joined([mine, *tail])
     if got is None:
         got = swapped(sent, axis, (even_a, odd_a))
@@ -327,7 +336,11 @@
                         x_ref[u, lo:hi, :], w, preferred_element_type=jnp.float32
                     ).astype(jnp.bfloat16)
                 part = feat // n_slots
-                per = n_slots // n_buffers
+                places = [
+                    (ref, n * 3 * part)
+                    for ref in w_refs
+                    for n in range(ref.shape[0] // (3 * part))
+                ]
                 acc = None
                 for t in range(0, n_slots, 2):
                     lhs = []
@@ -335,8 +348,8 @@
                     for s in (t, t + 1):
                         at = pl.multiple_of(device(slots[s]) * part, LANES)
                         lhs.append(x_ref[u, lo:hi, pl.ds(at, part)])
-                        top = (s % per * 3 + which) * part
-                        rhs.append(w_refs[s // per][top : top + part, :])
+                        ref, top = places[s]
+                        rhs.append(ref[top + which * part : top + (which + 1) * part, :])
                     one = jnp.dot(
                         jnp.concatenate(lhs, axis=1),
                         jnp.concatenate(rhs, axis=0),

time: 57.8 us -> 57.1 us (0.988)
  starting transfers between devices: 29 us -> 26 us
  waiting for transfers between devices: 8.53 us -> 10.5 us
    ppermute x17 -> x20, starting transfers between devices: 25.5 us -> 22.5 us  [swapped(): lax.ppermute(block, axis, [(i, i ^ masks[i % 2]) for i in range(count)])]
    ppermute x17 -> x20, waiting for transfers between devices: 8.53 us -> 10.5 us  [swapped(): lax.ppermute(block, axis, [(i, i ^ masks[i % 2]) for i in range(count)])]
  transfers between devices with their start and end apart: 18 -> 21, of which waited for: 4 -> 5; matrix products, arithmetic and copies ran while one was open for 0% -> 0% of each run, Pallas kernels for 20% -> 21%
where the time goes in v1:
time: 57.1 us; the launch traced here: 56 us
  starting transfers between devices  26 us (46%)
  Pallas kernels  17.8 us (31%)
  waiting for transfers between devices  10.5 us (18%)
  between operations  1.5 us (3%)
    ppermute x20, starting transfers between devices, swapped(): lax.ppermute(block, axis, [(i, i ^ masks[i % 2]) for i in range(count)])  22.5 us
    pallas_call x4, Pallas kernels, attend_chunk(): pl.pallas_call(make_kernel(dims, first, last, sliced, len(weights), colum...  14 us
    ppermute x20, waiting for transfers between devices, swapped(): lax.ppermute(block, axis, [(i, i ^ masks[i % 2]) for i in range(count)])  10.5 us
    ppermute x1, starting transfers between devices, local(): far = lax.ppermute(far_sent, 'seq', inner + [(b, a) for a, b in inner])  3.5 us
    pallas_call x1, Pallas kernels, prepare(): pl.pallas_call(kernel, in_specs=[pl.BlockSpec(memory_space=pltpu.SMEM)] *...  1.99 us
    pallas_call x1, Pallas kernels, cut(): pl.pallas_call(kernel, in_specs=[pl.BlockSpec(memory_space=pltpu.SMEM)] +...  1.75 us
  transfers between devices with their start and end apart: 21, of which 5 were waited for; matrix products, arithmetic and copies ran while one was open for 0% of the time, Pallas kernels for 21%

profile of v1, /device:TPU:3, one launch (start us, length us, event | category | flops | bytes accessed | tf_op | source)
XLA Modules:
  0.0 56.0 jit_solution(8498448517022056189)
XLA Ops:
  0.7 1.7 %cut.1 = (bf16[384,256]{1,0:T(8,128)(2,1)S(1)}, bf16[128,1024]{1,0:T(8,128)(2,1)S(1)}, bf16[128,1024]{1,0:T(8,128)(2,1)S(1)}, bf16[16,256]{1,0:T(8,128)(2,1)S(1)}) custom-call(s32[2]{0:T(128)S(1)} %pad_add_fusion.ids_ref.refs_0_, bf16[1,512,1024]{2,1,0:T(8,128)(2,1)} %frames_ref.1, bf16[1,4,1024]{2,1,0:T(4,128)(2,1)} %m_ref.1, bf16[1024,256]{1,0:T(8,128)(2,1)} %refs_2_.3, ...), custom_call_target="tpu_custom_call" | custom-call | tf_op jit(solution)/shard_map/cut/pallas_call | solution.py:116
  2.5 1.4 %collective-permute-start = (bf16[384,256]{1,0:T(8,128)(2,1)S(1)}, bf16[384,256]{1,0:T(8,128)(2,1)S(1)}, u32[]{:S(2)}, u32[]{:S(2)}) collective-permute-start(bf16[384,256]{1,0:T(8,128)(2,1)S(1)} %get-tuple-element.12), channel_id=1, source_target_pairs={{0,8},{8,0},{16,24},{24,16},{1,9},{9,1},{17,25},{25,17},{2,10},{10... | collective-permute-start | bytes 589832 | tf_op jit(solution)/shard_map/ppermute | solution.py:28
  3.9 2.3 %collective-permute-start.6 = (bf16[384,256]{1,0:T(8,128)(2,1)S(1)}, bf16[384,256]{1,0:T(8,128)(2,1)S(1)}, u32[]{:S(2)}, u32[]{:S(2)}) collective-permute-start(bf16[384,256]{1,0:T(8,128)(2,1)S(1)} %get-tuple-element.12), channel_id=1, source_target_pairs={{0,16},{8,24},{16,0},{24,8},{1,17},{9,25},{17,1},{25,9},{2,18},{10... | collective-permute-start | bytes 589832 | tf_op jit(solution)/shard_map/ppermute | solution.py:28
  6.2 1.2 %collective-permute-start.1 = (bf16[16,256]{1,0:T(8,128)(2,1)S(1)}, bf16[16,256]{1,0:T(8,128)(2,1)S(1)}, u32[]{:S(2)}, u32[]{:S(2)}) collective-permute-start(bf16[16,256]{1,0:T(8,128)(2,1)S(1)} %get-tuple-element.13), channel_id=1, source_target_pairs={{0,1},{1,0},{2,3},{3,2},{4,5},{5,4},{6,7},{7,6},{8,9},{9,8},{10,11... | collective-permute-start | bytes 24584 | tf_op jit(solution)/shard_map/ppermute | solution.py:28
  7.4 3.5 %collective-permute-start.5 = (bf16[128,1024]{1,0:T(8,128)(2,1)S(1)}, bf16[128,1024]{1,0:T(8,128)(2,1)S(1)}, u32[]{:S(2)}, u32[]{:S(2)}) collective-permute-start(bf16[128,1024]{1,0:T(8,128)(2,1)S(1)} %get-tuple-element.15), channel_id=1, source_target_pairs={{1,2},{3,4},{5,6},{2,1},{4,3},{6,5},{9,10},{11,12},{13,14},{10,9},... | collective-permute-start | bytes 786440 | tf_op jit(solution)/shard_map/ppermute | solution.py:602
  10.9 1.1 %collective-permute-done = bf16[384,256]{1,0:T(8,128)(2,1)S(1)} collective-permute-done((bf16[384,256]{1,0:T(8,128)(2,1)S(1)}, bf16[384,256]{1,0:T(8,128)(2,1)S(1)}, u32[]{:S(2)}, u32[]{:S(2)}) %collective-permute-start) | collective-permute-done | bytes 196640 | tf_op jit(solution)/shard_map/ppermute | solution.py:28
  12.1 1.3 %collective-permute-start.8 = (bf16[384,256]{1,0:T(8,128)(2,1)S(1)}, bf16[384,256]{1,0:T(8,128)(2,1)S(1)}, u32[]{:S(2)}, u32[]{:S(2)}) collective-permute-start(bf16[384,256]{1,0:T(8,128)(2,1)S(1)} %collective-permute-done.6), channel_id=1, source_target_pairs={{0,2},{1,5},{2,0},{3,7},{4,6},{5,1},{6,4},{7,3},{8,10},{9,13},{10,... | collective-permute-start | bytes 589832 | tf_op jit(solution)/shard_map/ppermute | solution.py:28
  13.4 0.2 collective-permute-start.2
  13.7 5.1 %collective-permute-done.8 = bf16[384,256]{1,0:T(8,128)(2,1)S(1)} collective-permute-done((bf16[384,256]{1,0:T(8,128)(2,1)S(1)}, bf16[384,256]{1,0:T(8,128)(2,1)S(1)}, u32[]{:S(2)}, u32[]{:S(2)}) %collective-permute-start.8) | collective-permute-done | bytes 196640 | tf_op jit(solution)/shard_map/ppermute | solution.py:28
  18.9 2.5 %collective-permute-done.2 = bf16[416,256]{1,0:T(8,128)(2,1)S(1)} collective-permute-done((bf16[416,256]{1,0:T(8,128)(2,1)S(1)}, bf16[416,256]{1,0:T(8,128)(2,1)S(1)}, u32[]{:S(2)}, u32[]{:S(2)}) %collective-permute-start.2) | collective-permute-done | bytes 213024 | tf_op jit(solution)/shard_map/ppermute | solution.py:28
  22.1 1.5 %collective-permute-start.7 = (bf16[384,256]{1,0:T(8,128)(2,1)S(1)}, bf16[384,256]{1,0:T(8,128)(2,1)S(1)}, u32[]{:S(2)}, u32[]{:S(2)}) collective-permute-start(bf16[384,256]{1,0:T(8,128)(2,1)S(1)} %collective-permute-done.6), channel_id=1, source_target_pairs={{0,8},{8,0},{16,24},{24,16},{1,9},{9,1},{17,25},{25,17},{2,10},{10... | collective-permute-start | bytes 589832 | tf_op jit(solution)/shard_map/ppermute | solution.py:28
  23.7 6.7 %collective-permute-start.19 = (bf16[768,256]{1,0:T(8,128)(2,1)S(1)}, bf16[768,256]{1,0:T(8,128)(2,1)S(1)}, u32[]{:S(2)}, u32[]{:S(2)}) collective-permute-start(bf16[768,256]{1,0:T(8,128)(2,1)S(1)} %constant_dynamic-update-slice_fusion.refs_3_), channel_id=1, source_target_pairs={{0,1},{1,0},{2,3},{3,2},{4,5},{5,4},{6,7},{7,6},{8,9},{9,8},{10,11... | collective-permute-start | bytes 1179656 | tf_op jit(solution)/shard_map/ppermute | solution.py:28
  30.3 0.3 collective-permute-start.20
  30.7 2.0 %prepare.1 = (bf16[1,720,1024]{2,1,0:T(8,128)(2,1)S(1)}, bf16[1,704,256]{2,1,0:T(8,128)(2,1)S(1)}, bf16[1,704,256]{2,1,0:T(8,128)(2,1)S(1)}, bf16[1,560,256]{2,1,0:T(8,128)(2,1)S(1)}) custom-call(s32[2]{0:T(128)S(1)} %pad_add_fusion.ids_ref.refs_0_, s32[1]{0:T(128)S(6)} %copy.17.len_ref.refs_1_, bf16[1,512,1024]{2,1,0:T(8,128)(2,1)S(1)} %copy-done, ...), custom_call_target="tpu_custom_call" | custom-call | flops 4127195136 | bytes 1441792 | tf_op jit(solution)/shard_map/prepare/pallas_call | solution.py:482
  32.7 1.4 %collective-permute-start.9 = (bf16[384,256]{1,0:T(8,128)(2,1)S(1)}, bf16[384,256]{1,0:T(8,128)(2,1)S(1)}, u32[]{:S(2)}, u32[]{:S(2)}) collective-permute-start(bf16[384,256]{1,0:T(8,128)(2,1)S(1)} %collective-permute-done.8), channel_id=1, source_target_pairs={{0,8},{8,0},{16,24},{24,16},{1,9},{9,1},{17,25},{25,17},{2,10},{10... | collective-permute-start | bytes 589832 | tf_op jit(solution)/shard_map/ppermute | solution.py:28
  34.2 1.8 %collective-permute-start.16 = (bf16[832,256]{1,0:T(8,128)(2,1)S(1)}, bf16[832,256]{1,0:T(8,128)(2,1)S(1)}, u32[]{:S(2)}, u32[]{:S(2)}) collective-permute-start(bf16[832,256]{1,0:T(8,128)(2,1)S(1)} %slice_dynamic-update-slice_fusion.1.refs_2_.refs_3_), channel_id=1, source_target_pairs={{0,1},{1,0},{2,3},{3,2},{4,5},{5,4},{6,7},{7,6},{8,9},{9,8},{10,11... | collective-permute-start | bytes 1277960 | tf_op jit(solution)/shard_map/ppermute | solution.py:28
  36.0 2.4 %attend_first.1 = (bf16[1,528,256]{2,1,0:T(8,128)(2,1)S(1)}, bf16[1,720,1024]{2,1,0:T(8,128)(2,1)S(1)}) custom-call(s32[2]{0:T(128)S(1)} %pad_add_fusion.ids_ref.refs_0_, s32[1]{0:T(128)S(6)} %copy.17.len_ref.refs_1_, bf16[832,256]{1,0:T(8,128)(2,1)S(1)} %slice_dynamic-update-slice_fusion.1.refs_2_.refs_3_, ...), custom_call_target="tpu_custom_call", output_to_operand_aliasing={{1}: (4, {})} | custom-call | flops 4127195136 | bytes 1441792 | tf_op jit(solution)/shard_map/attend_first/pallas_call | solution.py:556
  38.3 0.8 %collective-permute-done.9.refs_4_ = bf16[384,256]{1,0:T(8,128)(2,1)S(1)} collective-permute-done((bf16[384,256]{1,0:T(8,128)(2,1)S(1)}, bf16[384,256]{1,0:T(8,128)(2,1)S(1)}, u32[]{:S(2)}, u32[]{:S(2)}) %collective-permute-start.9) | collective-permute-done | bytes 196640 | tf_op jit(solution)/shard_map/ppermute | solution.py:28
  39.1 3.0 %collective-permute-start.12 = (bf16[384,256]{1,0:T(8,128)(2,1)S(1)}, bf16[384,256]{1,0:T(8,128)(2,1)S(1)}, u32[]{:S(2)}, u32[]{:S(2)}) collective-permute-start(bf16[384,256]{1,0:T(8,128)(2,1)S(1)} %collective-permute-done.7.refs_3_), channel_id=1, source_target_pairs={{0,1},{1,0},{2,3},{3,2},{4,5},{5,4},{6,7},{7,6},{8,9},{9,8},{10,11... | collective-permute-start | bytes 589832 | tf_op jit(solution)/shard_map/ppermute | solution.py:28
  42.2 3.6 %attend_next.4.refs_13_ = bf16[1,528,256]{2,1,0:T(8,128)(2,1)S(1)} custom-call(s32[2]{0:T(128)S(1)} %pad_add_fusion.ids_ref.refs_0_, s32[1]{0:T(128)S(6)} %copy.17.len_ref.refs_1_, bf16[1,720,1024]{2,1,0:T(8,128)(2,1)S(1)} %get-tuple-element.20.refs_2_, bf16[768,256]{1,0:T(8,128)(2,1)S(1)} %constant_dynamic-update-slice_fusion.refs_3_, ...), custom_call_target="tpu_custom_call" | custom-call | flops 4127195136 | bytes 1441792 | tf_op jit(solution)/shard_map/attend_next/pallas_call | solution.py:556
  46.0 1.0 %collective-permute-done.11.refs_6_ = bf16[384,256]{1,0:T(8,128)(2,1)S(1)} collective-permute-done((bf16[384,256]{1,0:T(8,128)(2,1)S(1)}, bf16[384,256]{1,0:T(8,128)(2,1)S(1)}, u32[]{:S(2)}, u32[]{:S(2)}) %collective-permute-start.11) | collective-permute-done | bytes 196640 | tf_op jit(solution)/shard_map/ppermute | solution.py:28
  47.0 1.0 %collective-permute-start.14 = (bf16[384,256]{1,0:T(8,128)(2,1)S(1)}, bf16[384,256]{1,0:T(8,128)(2,1)S(1)}, u32[]{:S(2)}, u32[]{:S(2)}) collective-permute-start(bf16[384,256]{1,0:T(8,128)(2,1)S(1)} %collective-permute-done.10.refs_5_), channel_id=1, source_target_pairs={{0,1},{1,0},{2,3},{3,2},{4,5},{5,4},{6,7},{7,6},{8,9},{9,8},{10,11... | collective-permute-start | bytes 589832 | tf_op jit(solution)/shard_map/ppermute | solution.py:28
  47.9 3.6 %attend_next.3.refs_12_ = bf16[1,528,256]{2,1,0:T(8,128)(2,1)S(1)} custom-call(s32[2]{0:T(128)S(1)} %pad_add_fusion.ids_ref.refs_0_, s32[1]{0:T(128)S(6)} %copy.17.len_ref.refs_1_, bf16[1,720,1024]{2,1,0:T(8,128)(2,1)S(1)} %get-tuple-element.20.refs_2_, bf16[832,256]{1,0:T(8,128)(2,1)S(1)} %slice_dynamic-update-slice_fusion.1.refs_2_.refs_3_, ...), custom_call_target="tpu_custom_call" | custom-call | flops 4127195136 | bytes 1441792 | tf_op jit(solution)/shard_map/attend_next/pallas_call | solution.py:556
  51.6 4.4 %attend_next.5 = (bf16[1,512,1024]{2,1,0:T(8,128)(2,1)}, bf16[1,4,1024]{2,1,0:T(4,128)(2,1)}) custom-call(s32[2]{0:T(128)S(1)} %pad_add_fusion.ids_ref.refs_0_, s32[1]{0:T(128)S(6)} %copy.17.len_ref.refs_1_, bf16[1,720,1024]{2,1,0:T(8,128)(2,1)S(1)} %get-tuple-element.20.refs_2_, bf16[384,256]{1,0:T(8,128)(2,1)S(1)} %collective-permute-done.7.refs_3_, ...), custom_call_target="tpu_custom_call" | custom-call | flops 4127195136 | bytes 1441792 | tf_op jit(solution)/shard_map/attend_next/pallas_call | solution.py:556
  (43 shorter events, 0.6 us)
Async XLA Ops:
  0.7 30.0 %copy-start.3 = (bf16[1024,256]{1,0:T(8,128)(2,1)S(1)}, bf16[1024,256]{1,0:T(8,128)(2,1)}, u32[]{:S(2)}) copy-start(bf16[1024,256]{1,0:T(8,128)(2,1)} %refs_9_.1) | copy-start | bytes 1572868
  2.5 28.2 %copy-start = (bf16[1,512,1024]{2,1,0:T(8,128)(2,1)S(1)}, bf16[1,512,1024]{2,1,0:T(8,128)(2,1)}, u32[]{:S(2)}) copy-start(bf16[1,512,1024]{2,1,0:T(8,128)(2,1)} %frames_ref.1) | copy-start | bytes 3145732
  2.5 28.2 %copy-start.1 = (bf16[1024,256]{1,0:T(8,128)(2,1)S(1)}, bf16[1024,256]{1,0:T(8,128)(2,1)}, u32[]{:S(2)}) copy-start(bf16[1024,256]{1,0:T(8,128)(2,1)} %refs_2_.3) | copy-start | bytes 1572868
  2.5 9.5 %collective-permute-start = (bf16[384,256]{1,0:T(8,128)(2,1)S(1)}, bf16[384,256]{1,0:T(8,128)(2,1)S(1)}, u32[]{:S(2)}, u32[]{:S(2)}) collective-permute-start(bf16[384,256]{1,0:T(8,128)(2,1)S(1)} %get-tuple-element.12), channel_id=1, source_target_pairs={{0,8},{8,0},{16,24},{24,16},{1,9},{9,1},{17,25},{25,17},{2,10},{10... | collective-permute-start | bytes 589832 | tf_op jit(solution)/shard_map/ppermute | solution.py:28
  3.9 8.2 %collective-permute-start.6 = (bf16[384,256]{1,0:T(8,128)(2,1)S(1)}, bf16[384,256]{1,0:T(8,128)(2,1)S(1)}, u32[]{:S(2)}, u32[]{:S(2)}) collective-permute-start(bf16[384,256]{1,0:T(8,128)(2,1)S(1)} %get-tuple-element.12), channel_id=1, source_target_pairs={{0,16},{8,24},{16,0},{24,8},{1,17},{9,25},{17,1},{25,9},{2,18},{10... | collective-permute-start | bytes 589832 | tf_op jit(solution)/shard_map/ppermute | solution.py:28
  6.2 7.2 %collective-permute-start.1 = (bf16[16,256]{1,0:T(8,128)(2,1)S(1)}, bf16[16,256]{1,0:T(8,128)(2,1)S(1)}, u32[]{:S(2)}, u32[]{:S(2)}) collective-permute-start(bf16[16,256]{1,0:T(8,128)(2,1)S(1)} %get-tuple-element.13), channel_id=1, source_target_pairs={{0,1},{1,0},{2,3},{3,2},{4,5},{5,4},{6,7},{7,6},{8,9},{9,8},{10,11... | collective-permute-start | bytes 24584 | tf_op jit(solution)/shard_map/ppermute | solution.py:28
  7.4 16.3 %collective-permute-start.4 = (bf16[128,1024]{1,0:T(8,128)(2,1)S(1)}, bf16[128,1024]{1,0:T(8,128)(2,1)S(1)}, u32[]{:S(2)}, u32[]{:S(2)}) collective-permute-start(bf16[128,1024]{1,0:T(8,128)(2,1)S(1)} %get-tuple-element.14), channel_id=1, source_target_pairs={{0,1},{1,0},{2,3},{3,2},{4,5},{5,4},{6,7},{7,6},{8,9},{9,8},{10,11... | collective-permute-start | bytes 786440 | tf_op jit(solution)/shard_map/ppermute | solution.py:28
  7.4 23.3 %collective-permute-start.5 = (bf16[128,1024]{1,0:T(8,128)(2,1)S(1)}, bf16[128,1024]{1,0:T(8,128)(2,1)S(1)}, u32[]{:S(2)}, u32[]{:S(2)}) collective-permute-start(bf16[128,1024]{1,0:T(8,128)(2,1)S(1)} %get-tuple-element.15), channel_id=1, source_target_pairs={{1,2},{3,4},{5,6},{2,1},{4,3},{6,5},{9,10},{11,12},{13,14},{10,9},... | collective-permute-start | bytes 786440 | tf_op jit(solution)/shard_map/ppermute | solution.py:602
  12.1 6.7 %collective-permute-start.8 = (bf16[384,256]{1,0:T(8,128)(2,1)S(1)}, bf16[384,256]{1,0:T(8,128)(2,1)S(1)}, u32[]{:S(2)}, u32[]{:S(2)}) collective-permute-start(bf16[384,256]{1,0:T(8,128)(2,1)S(1)} %collective-permute-done.6), channel_id=1, source_target_pairs={{0,2},{1,5},{2,0},{3,7},{4,6},{5,1},{6,4},{7,3},{8,10},{9,13},{10,... | collective-permute-start | bytes 589832 | tf_op jit(solution)/shard_map/ppermute | solution.py:28
  13.4 8.0 %collective-permute-start.2 = (bf16[416,256]{1,0:T(8,128)(2,1)S(1)}, bf16[416,256]{1,0:T(8,128)(2,1)S(1)}, u32[]{:S(2)}, u32[]{:S(2)}) collective-permute-start(bf16[416,256]{1,0:T(8,128)(2,1)S(1)} %constant_dynamic-update-slice_fusion.4), channel_id=1, source_target_pairs={{0,2},{1,5},{2,0},{3,7},{4,6},{5,1},{6,4},{7,3},{8,10},{9,13},{10,... | collective-permute-start | bytes 638984 | tf_op jit(solution)/shard_map/ppermute | solution.py:28
  18.8 11.5 %collective-permute-start.18 = (bf16[768,256]{1,0:T(8,128)(2,1)S(1)}, bf16[768,256]{1,0:T(8,128)(2,1)S(1)}, u32[]{:S(2)}, u32[]{:S(2)}) collective-permute-start(bf16[768,256]{1,0:T(8,128)(2,1)S(1)} %constant_dynamic-update-slice_fusion.refs_3_), channel_id=1, source_target_pairs={{0,4},{1,3},{2,6},{3,1},{4,0},{5,7},{6,2},{7,5},{8,12},{9,11},{10,... | collective-permute-start | bytes 1179656 | tf_op jit(solution)/shard_map/ppermute | solution.py:28
  21.4 14.5 %collective-permute-start.3 = (bf16[832,256]{1,0:T(8,128)(2,1)S(1)}, bf16[832,256]{1,0:T(8,128)(2,1)S(1)}, u32[]{:S(2)}, u32[]{:S(2)}) collective-permute-start(bf16[832,256]{1,0:T(8,128)(2,1)S(1)} %slice_dynamic-update-slice_fusion.1.refs_2_.refs_3_), channel_id=1, source_target_pairs={{0,4},{1,3},{2,6},{3,1},{4,0},{5,7},{6,2},{7,5},{8,12},{9,11},{10,... | collective-permute-start | bytes 1277960 | tf_op jit(solution)/shard_map/ppermute | solution.py:28
  22.1 12.0 %collective-permute-start.7 = (bf16[384,256]{1,0:T(8,128)(2,1)S(1)}, bf16[384,256]{1,0:T(8,128)(2,1)S(1)}, u32[]{:S(2)}, u32[]{:S(2)}) collective-permute-start(bf16[384,256]{1,0:T(8,128)(2,1)S(1)} %collective-permute-done.6), channel_id=1, source_target_pairs={{0,8},{8,0},{16,24},{24,16},{1,9},{9,1},{17,25},{25,17},{2,10},{10... | collective-permute-start | bytes 589832 | tf_op jit(solution)/shard_map/ppermute | solution.py:28
  23.7 15.5 %collective-permute-start.19 = (bf16[768,256]{1,0:T(8,128)(2,1)S(1)}, bf16[768,256]{1,0:T(8,128)(2,1)S(1)}, u32[]{:S(2)}, u32[]{:S(2)}) collective-permute-start(bf16[768,256]{1,0:T(8,128)(2,1)S(1)} %constant_dynamic-update-slice_fusion.refs_3_), channel_id=1, source_target_pairs={{0,1},{1,0},{2,3},{3,2},{4,5},{5,4},{6,7},{7,6},{8,9},{9,8},{10,11... | collective-permute-start | bytes 1179656 | tf_op jit(solution)/shard_map/ppermute | solution.py:28
  30.3 11.8 %collective-permute-start.20 = (bf16[768,256]{1,0:T(8,128)(2,1)S(1)}, bf16[768,256]{1,0:T(8,128)(2,1)S(1)}, u32[]{:S(2)}, u32[]{:S(2)}) collective-permute-start(bf16[768,256]{1,0:T(8,128)(2,1)S(1)} %collective-permute-done.18.refs_4_), channel_id=1, source_target_pairs={{0,1},{1,0},{2,3},{3,2},{4,5},{5,4},{6,7},{7,6},{8,9},{9,8},{10,11... | collective-permute-start | bytes 1179656 | tf_op jit(solution)/shard_map/ppermute | solution.py:28
  32.7 6.4 %collective-permute-start.9 = (bf16[384,256]{1,0:T(8,128)(2,1)S(1)}, bf16[384,256]{1,0:T(8,128)(2,1)S(1)}, u32[]{:S(2)}, u32[]{:S(2)}) collective-permute-start(bf16[384,256]{1,0:T(8,128)(2,1)S(1)} %collective-permute-done.8), channel_id=1, source_target_pairs={{0,8},{8,0},{16,24},{24,16},{1,9},{9,1},{17,25},{25,17},{2,10},{10... | collective-permute-start | bytes 589832 | tf_op jit(solution)/shard_map/ppermute | solution.py:28
  34.2 13.7 %collective-permute-start.16 = (bf16[832,256]{1,0:T(8,128)(2,1)S(1)}, bf16[832,256]{1,0:T(8,128)(2,1)S(1)}, u32[]{:S(2)}, u32[]{:S(2)}) collective-permute-start(bf16[832,256]{1,0:T(8,128)(2,1)S(1)} %slice_dynamic-update-slice_fusion.1.refs_2_.refs_3_), channel_id=1, source_target_pairs={{0,1},{1,0},{2,3},{3,2},{4,5},{5,4},{6,7},{7,6},{8,9},{9,8},{10,11... | collective-permute-start | bytes 1277960 | tf_op jit(solution)/shard_map/ppermute | solution.py:28
  36.0 12.0 %collective-permute-start.17 = (bf16[832,256]{1,0:T(8,128)(2,1)S(1)}, bf16[832,256]{1,0:T(8,128)(2,1)S(1)}, u32[]{:S(2)}, u32[]{:S(2)}) collective-permute-start(bf16[832,256]{1,0:T(8,128)(2,1)S(1)} %collective-permute-done.3.refs_3_.refs_4_), channel_id=1, source_target_pairs={{0,1},{1,0},{2,3},{3,2},{4,5},{5,4},{6,7},{7,6},{8,9},{9,8},{10,11... | collective-permute-start | bytes 1277960 | tf_op jit(solution)/shard_map/ppermute | solution.py:28
  39.1 6.7 %collective-permute-start.10 = (bf16[384,256]{1,0:T(8,128)(2,1)S(1)}, bf16[384,256]{1,0:T(8,128)(2,1)S(1)}, u32[]{:S(2)}, u32[]{:S(2)}) collective-permute-start(bf16[384,256]{1,0:T(8,128)(2,1)S(1)} %collective-permute-done.7.refs_3_), channel_id=1, source_target_pairs={{0,4},{1,3},{2,6},{3,1},{4,0},{5,7},{6,2},{7,5},{8,12},{9,11},{10,... | collective-permute-start | bytes 589832 | tf_op jit(solution)/shard_map/ppermute | solution.py:28
  39.1 12.4 %collective-permute-start.12 = (bf16[384,256]{1,0:T(8,128)(2,1)S(1)}, bf16[384,256]{1,0:T(8,128)(2,1)S(1)}, u32[]{:S(2)}, u32[]{:S(2)}) collective-permute-start(bf16[384,256]{1,0:T(8,128)(2,1)S(1)} %collective-permute-done.7.refs_3_), channel_id=1, source_target_pairs={{0,1},{1,0},{2,3},{3,2},{4,5},{5,4},{6,7},{7,6},{8,9},{9,8},{10,11... | collective-permute-start | bytes 589832 | tf_op jit(solution)/shard_map/ppermute | solution.py:28
  42.1 4.8 %collective-permute-start.11 = (bf16[384,256]{1,0:T(8,128)(2,1)S(1)}, bf16[384,256]{1,0:T(8,128)(2,1)S(1)}, u32[]{:S(2)}, u32[]{:S(2)}) collective-permute-start(bf16[384,256]{1,0:T(8,128)(2,1)S(1)} %collective-permute-done.9.refs_4_), channel_id=1, source_target_pairs={{0,4},{1,3},{2,6},{3,1},{4,0},{5,7},{6,2},{7,5},{8,12},{9,11},{10,... | collective-permute-start | bytes 589832 | tf_op jit(solution)/shard_map/ppermute | solution.py:28
  45.8 5.8 %collective-permute-start.13 = (bf16[384,256]{1,0:T(8,128)(2,1)S(1)}, bf16[384,256]{1,0:T(8,128)(2,1)S(1)}, u32[]{:S(2)}, u32[]{:S(2)}) collective-permute-start(bf16[384,256]{1,0:T(8,128)(2,1)S(1)} %collective-permute-done.9.refs_4_), channel_id=1, source_target_pairs={{0,1},{1,0},{2,3},{3,2},{4,5},{5,4},{6,7},{7,6},{8,9},{9,8},{10,11... | collective-permute-start | bytes 589832 | tf_op jit(solution)/shard_map/ppermute | solution.py:28
  47.0 4.6 %collective-permute-start.14 = (bf16[384,256]{1,0:T(8,128)(2,1)S(1)}, bf16[384,256]{1,0:T(8,128)(2,1)S(1)}, u32[]{:S(2)}, u32[]{:S(2)}) collective-permute-start(bf16[384,256]{1,0:T(8,128)(2,1)S(1)} %collective-permute-done.10.refs_5_), channel_id=1, source_target_pairs={{0,1},{1,0},{2,3},{3,2},{4,5},{5,4},{6,7},{7,6},{8,9},{9,8},{10,11... | collective-permute-start | bytes 589832 | tf_op jit(solution)/shard_map/ppermute | solution.py:28
  47.9 3.7 %collective-permute-start.15 = (bf16[384,256]{1,0:T(8,128)(2,1)S(1)}, bf16[384,256]{1,0:T(8,128)(2,1)S(1)}, u32[]{:S(2)}, u32[]{:S(2)}) collective-permute-start(bf16[384,256]{1,0:T(8,128)(2,1)S(1)} %collective-permute-done.11.refs_6_), channel_id=1, source_target_pairs={{0,1},{1,0},{2,3},{3,2},{4,5},{5,4},{6,7},{7,6},{8,9},{9,8},{10,11... | collective-permute-start | bytes 589832 | tf_op jit(solution)/shard_map/ppermute | solution.py:28
  (1 other events, 28.2 us)
